TPU v7x, 1024 devices: a whole 4x8x16 slice. The times are simulated.
1024 devices in a mesh: ctx: 32 (over y, x), head: 32 (over z, core).
Axes of the slice: x: 4, y: 8, z: 16, core: 2. Of those that a mesh axis runs over, the one named last changes fastest.
Arguments:
- query_rows: bfloat16 [49152, 4096], P(('ctx', 'head')), may hold values from -6 to 6
- key_rows: bfloat16 [49152, 4096], P(('ctx', 'head')), may hold values from -6 to 6
- value_rows: bfloat16 [49152, 4096], P('ctx', 'head'), may hold values from -6 to 6
- out_grad: bfloat16 [49152, 4096], P('ctx', 'head'), may hold values from -6 to 6
- entry_state: float32 [32, 128, 128], P('head'), may hold values from -1330.215 to 1330.215
Outputs:
- attended: bfloat16 [49152, 4096], P(('ctx', 'head'))
- query_grad: bfloat16 [49152, 4096], P('ctx', 'head')
- key_grad: bfloat16 [49152, 4096], P('ctx', 'head')
- value_grad: bfloat16 [49152, 4096], P('ctx', 'head')
- state_grad: float32 [32, 128, 128], P('head')
All inputs are finite; a program needn't handle non-finite values.
Results may differ from a plain program's by a relative error of at most 0.0049.
Values may be sent and summed in bfloat16 or wider, within the bound.
A program may use at most 32 MiB of HBM per device.

v0:
```python
import math

import jax
import jax.numpy as jnp
from jax import lax
from jax.sharding import Mesh
from jax.sharding import PartitionSpec as P

SPAN = 384
CTX = ("ctx_0", "ctx_1")
HEAD = ("head_0", "head_1")
CTX_HEAD = ("ctx_0", "ctx_1", "head_0", "head_1")


def copy_for_each(shard, axis):
    devices = lax.axis_size(axis)
    return lax.all_to_all(
        jnp.broadcast_to(shard[None], (devices, *shard.shape)), axis, 0, 0, tiled=True
    )


def of_everyone(shard, axis):
    return copy_for_each(shard, axis).sum(axis=0)


def nothing_yet(shard, identity):
    return jax.tree.map(
        lambda part, zero: jnp.zeros_like(part) + jnp.asarray(zero, part.dtype), shard, identity
    )


def carried_in(shard, axes, combine, identity):
    before = start = nothing_yet(shard, identity)
    subtotal = shard
    for axis in reversed(axes):
        devices, position = (lax.axis_size(axis), lax.axis_index(axis))
        pieces = jax.tree.map(lambda part: lax.all_gather(part, axis), subtotal)
        inside, subtotal = (start, start)
        for k in range(devices):
            passed = k < position
            subtotal = combine(subtotal, jax.tree.map(lambda part: part[k], pieces))
            inside = jax.tree.map(lambda new, old: jnp.where(passed, new, old), subtotal, inside)
        before = combine(inside, before)
    return before


def in_blocks(shard, dim, devices):
    before, after = (shard.shape[:dim], shard.shape[dim + 1 :])
    return jnp.moveaxis(shard.reshape(*before, devices, -1, *after), dim, 0)


def laid_out(tiles, dim):
    tiles = jnp.moveaxis(tiles, 0, dim)
    lengths = tiles.shape
    return tiles.reshape(*lengths[:dim], lengths[dim] * lengths[dim + 1], *lengths[dim + 2 :])


def moved_by_axis(tiles, axes, order):
    inside = tiles.shape[1:]
    filled = tiles.reshape(*(lax.axis_size(a) for a in axes), *inside)
    for k in order:
        filled = lax.all_to_all(filled, axes[k], k, k, tiled=True)
    return filled.reshape(-1, *inside)


def exchange_by_chip(shard, groups, order, split_dim, concat_dim):
    devices = lax.axis_size(groups[0]) * lax.axis_size(groups[1])
    tiles = in_blocks(shard, split_dim, devices)
    return laid_out(moved_by_axis(tiles, groups, order), concat_dim)


def add_states(earlier, later):
    return jax.tree.map(jnp.add, earlier, later)


def local(query_rows, key_rows, value_rows, out_grad, entry_state):
    heads_local = entry_state.shape[0]
    head_dim = entry_state.shape[1]
    length = value_rows.shape[0]
    width_local = value_rows.shape[1]
    blocks = length // SPAN
    scale = 1.0 / math.sqrt(head_dim * length * lax.axis_size(CTX))
    shape4 = (blocks, SPAN, heads_local, head_dim)
    value_block = value_rows.reshape(shape4)
    grad_block = out_grad.reshape(shape4)
    query_ex, key_ex = (
        lax.all_to_all(query_rows, HEAD, split_axis=1, concat_axis=0, tiled=True),
        lax.all_to_all(key_rows, HEAD, split_axis=1, concat_axis=0, tiled=True),
    )
    query_block = query_ex.reshape(shape4)
    key_block = key_ex.reshape(shape4)
    own_kv = jnp.einsum(
        "bchd,bche->bhde", key_block, value_block, preferred_element_type=jnp.float32
    )
    own_qg = jnp.einsum(
        "bchd,bche->bhde", query_block, grad_block, preferred_element_type=jnp.float32
    )
    kv_total = jnp.sum(own_kv, axis=0)
    qg_total = jnp.sum(own_qg, axis=0)
    zero_state = jnp.zeros_like(kv_total)
    grand = of_everyone(qg_total, CTX)
    before, before_qg = carried_in((kv_total, qg_total), CTX, add_states, (zero_state, zero_state))
    after = grand - before_qg - qg_total
    state_in = entry_state + before
    prefix_kv = jnp.concatenate([zero_state[None], jnp.cumsum(own_kv[:-1], axis=0)], axis=0)
    states = (state_in[None] + prefix_kv).astype(jnp.bfloat16)
    suffix_incl = jnp.flip(jnp.cumsum(jnp.flip(own_qg, 0), axis=0), 0)
    suffix_qg = jnp.concatenate([suffix_incl[1:], zero_state[None]], axis=0)
    adjoints = (after[None] + suffix_qg).astype(jnp.bfloat16)
    positions = jnp.arange(SPAN)
    causal = (positions[:, None] >= positions[None, :])[None, None]
    scores = jnp.where(
        causal,
        jnp.einsum("bchd,bshd->bhcs", query_block, key_block, preferred_element_type=jnp.float32),
        0.0,
    ).astype(jnp.bfloat16)
    errors = jnp.where(
        causal,
        jnp.einsum("bche,bshe->bhcs", grad_block, value_block, preferred_element_type=jnp.float32),
        0.0,
    ).astype(jnp.bfloat16)
    attended = scale * (
        jnp.einsum("bchd,bhde->bche", query_block, states, preferred_element_type=jnp.float32)
        + jnp.einsum("bhcs,bshe->bche", scores, value_block, preferred_element_type=jnp.float32)
    )
    attended = attended.astype(jnp.bfloat16).reshape(length, width_local)
    attended_tok = exchange_by_chip(attended, ("head_0", "head_1"), (1, 0), 0, 1)
    query_grad = scale * (
        jnp.einsum("bche,bhde->bchd", grad_block, states, preferred_element_type=jnp.float32)
        + jnp.einsum("bhcs,bshd->bchd", errors, key_block, preferred_element_type=jnp.float32)
    )
    key_grad = scale * (
        jnp.einsum("bche,bhde->bchd", value_block, adjoints, preferred_element_type=jnp.float32)
        + jnp.einsum("bhcs,bchd->bshd", errors, query_block, preferred_element_type=jnp.float32)
    )
    value_grad = scale * (
        jnp.einsum("bchd,bhde->bche", key_block, adjoints, preferred_element_type=jnp.float32)
        + jnp.einsum("bhcs,bche->bshe", scores, grad_block, preferred_element_type=jnp.float32)
    )
    query_grad = query_grad.astype(jnp.bfloat16).reshape(length, width_local)
    key_grad = key_grad.astype(jnp.bfloat16).reshape(length, width_local)
    value_grad = value_grad.astype(jnp.bfloat16).reshape(length, width_local)
    state_grad = scale * grand
    return (attended_tok, query_grad, key_grad, value_grad, state_grad)


def solution(mesh):
    split = Mesh(mesh.devices.reshape(8, 4, 16, 2), ("ctx_0", "ctx_1", "head_0", "head_1"))
    in_specs = (
        P(CTX_HEAD, None),
        P(CTX_HEAD, None),
        P(CTX, HEAD),
        P(CTX, HEAD),
        P(HEAD, None, None),
    )
    out_specs = (P(CTX_HEAD, None), P(CTX, HEAD), P(CTX, HEAD), P(CTX, HEAD), P(HEAD, None, None))
    return jax.shard_map(local, mesh=split, in_specs=in_specs, out_specs=out_specs, check_vma=False)
```

profile of v0, /device:TPU:94, one launch (start us, length us, event | category | flops | bytes accessed | tf_op | source)
XLA Modules:
  0.0 222.1 jit_solution(692672109207359520)
XLA Ops:
  0.6 0.0 copy-start
  0.7 1.9 copy_bitcast_fusion.2
  2.5 18.6 %all-to-all-start = ((bf16[48,32,128]{2,0,1:T(8,128)(2,1)}), bf16[48,32,128]{2,0,1:T(8,128)(2,1)S(1)}, u32[]{:S(2)}, u32[]{:S(2)}) async-start(bf16[48,32,128]{2,0,1:T(8,128)(2,1)} %copy_bitcast_fusion.2), calls=%async_computation | async-start | bytes 786432 | tf_op jit(solution)/shard_map/all_to_all | solution.py:88
  21.1 0.8 copy_bitcast_fusion.1
  21.9 25.8 %all-to-all-done = bf16[48,32,128]{2,0,1:T(8,128)(2,1)S(1)} async-done(((bf16[48,32,128]{2,0,1:T(8,128)(2,1)}), bf16[48,32,128]{2,0,1:T(8,128)(2,1)S(1)}, u32[]{:S(2)}, u32[]{:S(2)}) %all-to-all-start) | async-done | bytes 393248 | tf_op jit(solution)/shard_map/all_to_all | solution.py:88
  47.7 5.4 %all-to-all-start.1 = ((bf16[48,32,128]{2,0,1:T(8,128)(2,1)}), bf16[48,32,128]{2,0,1:T(8,128)(2,1)S(1)}, u32[]{:S(2)}, u32[]{:S(2)}) async-start(bf16[48,32,128]{2,0,1:T(8,128)(2,1)} %copy_bitcast_fusion.1), calls=%async_computation.1 | async-start | bytes 786432 | tf_op jit(solution)/shard_map/all_to_all | solution.py:87
  53.2 0.0 copy-start.13
  53.2 0.3 fusion.45
  53.5 12.4 %all-gather = f32[512,128]{1,0:T(8,128)S(1)} all-gather(f32[128,128]{1,0:T(8,128)S(1)} %get-tuple-element.5), channel_id=2, replica_groups=mesh['ctx_0'=8,'ctx_1'=4,'head_0'=16,'head_1'=2] {'ctx_1'}, dimensions={0}, use_global_device_ids=true | all-gather | bytes 327680 | tf_op jit(solution)/shard_map/all_gather | solution.py:37
  66.0 25.8 %all_gather.20 = f32[8,1,128,128]{3,2,1,0:T(8,128)S(1)} all-gather(f32[1,1,128,128]{3,2,1,0:T(8,128)S(1)} %fusion.32), channel_id=1, replica_groups=mesh['ctx_0'=8,'ctx_1'=4,'head_0'=16,'head_1'=2] {'ctx_0'}, dimensions={0}, use_global_device_ids=true | all-gather | bytes 589824 | tf_op jit(solution)/shard_map/all_gather | solution.py:37
  91.8 0.0 copy-start.14
  91.9 0.5 select_convert_fusion.1
  92.3 0.3 copy-done.14
  92.7 0.1 fusion.31
  92.7 0.3 fusion.39
  93.1 0.6 copy-done.1
  93.7 0.6 fusion.12
  94.2 0.2 copy.115
  94.5 0.0 copy-start.5
  94.5 4.2 %all_to_all.47 = bf16[16,2,48,128]{3,2,0,1:T(8,128)(2,1)S(1)} all-to-all(bf16[16,2,48,128]{3,2,0,1:T(8,128)(2,1)S(1)} %copy.116), channel_id=1, replica_groups=mesh['ctx_0'=8,'ctx_1'=4,'head_0'=16,'head_1'=2] {'head_1'}, dimensions={1} | all-to-all | bytes 786432 | tf_op jit(solution)/shard_map/all_to_all | solution.py:62
  98.7 0.8 copy.117
  99.5 11.9 %all-to-all-start.3 = ((bf16[16,2,48,128]{3,2,1,0:T(8,128)(2,1)}), bf16[16,2,48,128]{3,2,1,0:T(8,128)(2,1)S(1)}, u32[]{:S(2)}, u32[]{:S(2)}) async-start(bf16[16,2,48,128]{3,2,1,0:T(8,128)(2,1)} %copy.117), calls=%async_computation.3 | async-start | bytes 786432 | tf_op jit(solution)/shard_map/all_to_all | solution.py:62
  111.4 1.0 fusion.46
  112.4 21.1 %all-to-all-done.3 = bf16[16,2,48,128]{3,2,1,0:T(8,128)(2,1)S(1)} async-done(((bf16[16,2,48,128]{3,2,1,0:T(8,128)(2,1)}), bf16[16,2,48,128]{3,2,1,0:T(8,128)(2,1)S(1)}, u32[]{:S(2)}, u32[]{:S(2)}) %all-to-all-start.3) | async-done | bytes 393248 | tf_op jit(solution)/shard_map/all_to_all | solution.py:62
  133.5 1.6 broadcast_in_dim.37
  135.0 9.3 %all-to-all-start.4 = ((f32[32,1,128,128]{3,2,1,0:T(8,128)}), f32[32,1,128,128]{3,2,1,0:T(8,128)S(1)}, u32[]{:S(2)}, u32[]{:S(2)}) async-start(f32[32,1,128,128]{3,2,1,0:T(8,128)} %broadcast_in_dim.37), calls=%async_computation.4 | async-start | bytes 4194304 | tf_op jit(solution)/shard_map/all_to_all | solution.py:17
  144.4 2.5 %select_convert_fusion = bf16[4,384,384]{2,1,0:T(8,128)(2,1)} fusion(bf16[4,384,128]{2,1,0:T(8,128)(2,1)} %bitcast.163, bf16[4,384,128]{2,1,0:T(8,128)(2,1)S(1)} %bitcast.153, pred[384,384]{1,0:T(8,128)(4,1)} %copy-done.13), kind=kOutput, calls=%fused_computation | convolution fusion | flops 152174592 | bytes 2113536 | tf_op jit(solution)/shard_map/bche,bshe->bhcs/dot_general | solution.py:119
  146.9 1.7 reverse.4
  148.6 1.0 fusion.16
  149.6 0.7 slice.145
  150.3 1.6 slice.111
  151.9 1.4 fusion.37
  153.3 1.3 fusion.13
  154.6 1.9 copy.120
  156.5 13.1 %all-gather.1 = f32[512,128]{1,0:T(8,128)S(1)} all-gather(f32[128,128]{1,0:T(8,128)} %copy-done.10), channel_id=3, replica_groups=mesh['ctx_0'=8,'ctx_1'=4,'head_0'=16,'head_1'=2] {'ctx_1'}, dimensions={0}, use_global_device_ids=true | all-gather | bytes 327680 | tf_op jit(solution)/shard_map/all_gather | solution.py:37
  169.6 44.4 %all_gather.22 = f32[8,1,128,128]{3,2,1,0:T(8,128)} all-gather(f32[1,1,128,128]{3,2,1,0:T(8,128)S(1)} %fusion.26), channel_id=1, replica_groups=mesh['ctx_0'=8,'ctx_1'=4,'head_0'=16,'head_1'=2] {'ctx_0'}, dimensions={0}, use_global_device_ids=true | all-gather | bytes 589824 | tf_op jit(solution)/shard_map/all_gather | solution.py:37
  214.1 0.8 copy.145
  214.9 0.7 reduce_sum.31
  215.7 1.2 fusion.25
  216.9 0.0 copy-start.11
  216.9 0.0 copy-start.6
  216.9 1.4 fusion.33
  218.3 0.3 fusion.35
  218.6 0.6 multiply_bitcast_fusion
  219.2 0.5 fusion.15
  219.7 0.9 copy.128
  220.6 0.5 fusion.14
  221.1 0.9 copy.124
  (29 shorter events, 0.2 us)
Async XLA Ops:
  0.6 52.6 %copy-start = (bf16[1536,128]{1,0:T(8,128)(2,1)S(1)}, bf16[1536,128]{1,0:T(8,128)(2,1)}, u32[]{:S(2)}) copy-start(bf16[1536,128]{1,0:T(8,128)(2,1)} %param.7) | copy-start | bytes 1179652
  0.6 20.5 %copy-start.12 = (bf16[48,4096]{1,0:T(8,128)(2,1)S(1)}, bf16[48,4096]{1,0:T(8,128)(2,1)}, u32[]{:S(2)}) copy-start(bf16[48,4096]{1,0:T(8,128)(2,1)} %param.5) | copy-start | bytes 1179652
  2.5 45.2 %all-to-all-start = ((bf16[48,32,128]{2,0,1:T(8,128)(2,1)}), bf16[48,32,128]{2,0,1:T(8,128)(2,1)S(1)}, u32[]{:S(2)}, u32[]{:S(2)}) async-start(bf16[48,32,128]{2,0,1:T(8,128)(2,1)} %copy_bitcast_fusion.2), calls=%async_computation | async-start | bytes 786432 | tf_op jit(solution)/shard_map/all_to_all | solution.py:88
  47.7 44.1 %all-to-all-start.1 = ((bf16[48,32,128]{2,0,1:T(8,128)(2,1)}), bf16[48,32,128]{2,0,1:T(8,128)(2,1)S(1)}, u32[]{:S(2)}, u32[]{:S(2)}) async-start(bf16[48,32,128]{2,0,1:T(8,128)(2,1)} %copy_bitcast_fusion.1), calls=%async_computation.1 | async-start | bytes 786432 | tf_op jit(solution)/shard_map/all_to_all | solution.py:87
  53.2 38.7 %copy-start.13 = (pred[384,384]{1,0:T(8,128)(4,1)}, pred[384,384]{1,0:T(8,128)(4,1)S(1)}, u32[]{:S(2)}) copy-start(pred[384,384]{1,0:T(8,128)(4,1)S(1)} %iota_compare_fusion) | copy-start | bytes 442372
  91.8 0.8 copy-start.14
  92.7 1.0 copy-start.1
  94.5 16.9 %copy-start.5 = (bf16[1536,128]{1,0:T(8,128)(2,1)S(1)}, bf16[1536,128]{1,0:T(8,128)(2,1)}, u32[]{:S(2)}) copy-start(bf16[1536,128]{1,0:T(8,128)(2,1)} %param.8) | copy-start | bytes 1179652
  99.5 34.0 %all-to-all-start.3 = ((bf16[16,2,48,128]{3,2,1,0:T(8,128)(2,1)}), bf16[16,2,48,128]{3,2,1,0:T(8,128)(2,1)S(1)}, u32[]{:S(2)}, u32[]{:S(2)}) async-start(bf16[16,2,48,128]{3,2,1,0:T(8,128)(2,1)} %copy.117), calls=%async_computation.3 | async-start | bytes 786432 | tf_op jit(solution)/shard_map/all_to_all | solution.py:62
  112.4 22.6 %copy-start.10 = (f32[128,128]{1,0:T(8,128)}, f32[128,128]{1,0:T(8,128)S(1)}, u32[]{:S(2)}) copy-start(f32[128,128]{1,0:T(8,128)S(1)} %get-tuple-element.7) | copy-start | bytes 196612
  133.5 1.6 copy-start.8
  135.0 79.9 %all-to-all-start.4 = ((f32[32,1,128,128]{3,2,1,0:T(8,128)}), f32[32,1,128,128]{3,2,1,0:T(8,128)S(1)}, u32[]{:S(2)}, u32[]{:S(2)}) async-start(f32[32,1,128,128]{3,2,1,0:T(8,128)} %broadcast_in_dim.37), calls=%async_computation.4 | async-start | bytes 4194304 | tf_op jit(solution)/shard_map/all_to_all | solution.py:17
  151.9 1.4 copy-start.3
  156.5 57.6 %copy-start.9 = (bf16[16,2,48,128]{3,2,1,0:T(8,128)(2,1)S(1)}, bf16[16,2,48,128]{3,2,1,0:T(8,128)(2,1)}, u32[]{:S(2)}) copy-start(bf16[16,2,48,128]{3,2,1,0:T(8,128)(2,1)} %copy-done.8) | copy-start | bytes 1179652
  215.6 2.6 %copy-start.7 = (f32[3,1,128,128]{3,2,0,1:T(8,128)S(1)}, f32[3,1,128,128]{3,2,0,1:T(8,128)}, u32[]{:S(2)}) copy-start(f32[3,1,128,128]{3,2,0,1:T(8,128)} %slice.111) | copy-start | bytes 589828
  216.9 1.7 copy-start.11
  216.9 2.4 %copy-start.2 = (bf16[4,384,384]{2,1,0:T(8,128)(2,1)S(1)}, bf16[4,384,384]{2,1,0:T(8,128)(2,1)}, u32[]{:S(2)}) copy-start(bf16[4,384,384]{2,1,0:T(8,128)(2,1)} %copy-done.1) | copy-start | bytes 3538948
  216.9 2.4 %copy-start.6 = (bf16[1536,128]{1,0:T(8,128)(2,1)S(1)}, bf16[1536,128]{1,0:T(8,128)(2,1)}, u32[]{:S(2)}) copy-start(bf16[1536,128]{1,0:T(8,128)(2,1)} %param.8) | copy-start | bytes 1179652
  219.2 1.4 copy-start.4
where the time goes:
time: 223 us; the launch traced here: 222 us
  blocking collectives  100 us (45%)
  waiting for transfers between devices  46.8 us (21%)
  starting transfers between devices  45.2 us (20%)
  local copies, waits for them, and re-layouts  14.9 us (7%)
  matrix products  10.6 us (5%)
  other arithmetic  3.71 us (2%)
    all_gather x4, blocking collectives, carried_in(): pieces = jax.tree.map(lambda part: lax.all_gather(part, axis), subtotal)  95.8 us
    all_to_all x1, waiting for transfers between devices, local(): lax.all_to_all(key_rows, HEAD, split_axis=1, concat_axis=0, tiled=True)  25.8 us
    all_to_all x1, waiting for transfers between devices, moved_by_axis(): filled = lax.all_to_all(filled, axes[k], k, k, tiled=True)  21.1 us
    all_to_all x1, starting transfers between devices, local(): lax.all_to_all(key_rows, HEAD, split_axis=1, concat_axis=0, tiled=True)  18.6 us
    all_to_all x1, starting transfers between devices, moved_by_axis(): filled = lax.all_to_all(filled, axes[k], k, k, tiled=True)  11.9 us
    all_to_all x1, starting transfers between devices, copy_for_each(): lax.all_to_all(jnp.broadcast_to(shard[None], (devices, *shard.shape)), ax...  9.35 us
    all_to_all x1, starting transfers between devices, local(): lax.all_to_all(query_rows, HEAD, split_axis=1, concat_axis=0, tiled=True)  5.4 us
  transfers between devices with their start and end apart: 4, of which 2 were waited for; matrix products, arithmetic and copies ran while one was open for 7% of the time, Pallas kernels for 0%

commit v1 on v0

v1 whole, which is shorter than its diff:
```python
import functools
import math

import jax
import jax.numpy as jnp
from jax import lax
from jax.experimental import pallas as pl
from jax.experimental.pallas import tpu as pltpu
from jax.sharding import PartitionSpec as P

SPAN = 384
XS = 4
MESH = pl.DeviceIdType.MESH
F32 = jnp.float32
BF16 = jnp.bfloat16


def dot(a, b, ca, cb):
    return lax.dot_general(a, b, (((ca,), (cb,)), ((), ())), preferred_element_type=F32)


def kernel(
    cfg,
    q_hbm, k_hbm, v_hbm, g_hbm, s_hbm,
    att_out, qgrad_out, kgrad_out, vgrad_out, sgrad_out,
    k_send, q_send, k_all, q_all, v_all, g_all, s_own,
    att_send, att_recv,
    errors, scores, kv_blk, qg_blk, qgrad_part, kgrad_part, vgrad_part,
    own_quarter, row_in, row_sum, col_in, back_out, back_in,
    load_sem, send_sem, k_sem, q_sem, att_sem,
    ex_send, ex_recv,
):
    zs, ys, rows, dim, blocks, scale = cfg
    heads = 2 * zs
    per_block = SPAN // rows
    ctx = lax.axis_index("ctx")
    me = lax.axis_index("head")
    z = lax.div(me, 2)
    core = lax.rem(me, 2)
    y = lax.div(ctx, XS)
    x = lax.rem(ctx, XS)
    my_block = lax.div(me, per_block)
    my_rows = pl.ds(pl.multiple_of(me * rows, rows), rows)

    def columns(h):
        return pl.ds(pl.multiple_of(h * dim, dim), dim)

    def block_rows(b):
        return pl.ds(pl.multiple_of(b * SPAN, SPAN), SPAN)

    for src, dst, sem in ((k_hbm, k_send, 0), (q_hbm, q_send, 1)):
        @pl.loop(0, heads)
        def _(h):
            pltpu.make_async_copy(src.at[:, columns(h)], dst.at[h], load_sem.at[sem]).start()
    pltpu.make_async_copy(k_hbm.at[:, columns(me)], k_all.at[my_rows], k_sem.at[my_block]).start()
    pltpu.make_async_copy(q_hbm.at[:, columns(me)], q_all.at[my_rows], q_sem.at[my_block]).start()
    load_v = pltpu.make_async_copy(v_hbm, v_all, load_sem.at[2])
    load_g = pltpu.make_async_copy(g_hbm, g_all, load_sem.at[3])
    load_s = pltpu.make_async_copy(s_hbm, s_own, load_sem.at[4])
    load_v.start()
    load_g.start()
    load_s.start()

    barrier = pltpu.get_barrier_semaphore()

    @pl.loop(1, heads)
    def _(i):
        pl.semaphore_signal(
            barrier, inc=1, device_id={"head": lax.rem(me + i, heads)}, device_id_type=MESH
        )

    @pl.loop(1, XS)
    def _(i):
        pl.semaphore_signal(
            barrier, inc=1, device_id={"ctx": y * XS + lax.rem(x + i, XS)}, device_id_type=MESH
        )

    @pl.loop(1, ys)
    def _(i):
        pl.semaphore_signal(
            barrier, inc=1, device_id={"ctx": lax.rem(y + i, ys) * XS + x}, device_id_type=MESH
        )

    pltpu.make_async_copy(k_send, k_send, load_sem.at[0]).wait()
    pltpu.make_async_copy(q_send, q_send, load_sem.at[1]).wait()
    load_v.wait()
    load_g.wait()
    load_s.wait()
    pl.semaphore_wait(barrier, heads - 1 + XS - 1 + ys - 1)

    def post(src, dst, sem, recv, peer):
        pltpu.make_async_remote_copy(
            src_ref=src.at[peer], dst_ref=dst.at[my_rows], send_sem=send_sem.at[sem],
            recv_sem=recv.at[my_block], device_id={"head": peer}, device_id_type=MESH,
        ).start()

    for src, dst, sem, recv in ((k_send, k_all, 0, k_sem), (q_send, q_all, 1, q_sem)):
        post(src, dst, sem, recv, 2 * z + 1 - core)

        @pl.loop(1, zs)
        def _(i):
            step = lax.div(i + 1, 2) * (2 * lax.rem(i, 2) - 1)
            peer_z = lax.rem(z + step + zs, zs)
            post(src, dst, sem, recv, 2 * peer_z + core)
            post(src, dst, sem, recv, 2 * peer_z + 1 - core)

    causal = lax.broadcasted_iota(jnp.int32, (SPAN, SPAN), 0) >= lax.broadcasted_iota(
        jnp.int32, (SPAN, SPAN), 1
    )

    @pl.loop(0, blocks)
    def _(b):
        at = block_rows(b)
        errors[b] = jnp.where(causal, dot(g_all[at], v_all[at], 1, 1), 0.0).astype(BF16)

    for b in range(blocks):
        pltpu.make_async_copy(
            k_all.at[pl.ds(b * SPAN, SPAN)], k_all.at[pl.ds(b * SPAN, SPAN)], k_sem.at[b]
        ).wait()

    quarter = dim // XS

    def send_x(which, src_of, dst, i):
        to = lax.rem(x + i, XS)
        pltpu.make_async_remote_copy(
            src_ref=src_of(to), dst_ref=dst, send_sem=ex_send.at[which],
            recv_sem=ex_recv.at[which], device_id={"ctx": y * XS + to}, device_id_type=MESH,
        ).start()

    def stage_quarters(n, total):
        own_quarter[n] = total.reshape(XS, quarter, dim)
        for i in range(1, XS):
            send_x(3 * n, lambda to: own_quarter.at[n, to], row_in.at[n, x], i)
        row_in[n, x] = own_quarter[n, x]

    def stage_rows(n):
        three = row_in.at[n, pl.ds(0, XS - 1)]
        pltpu.make_async_copy(three, three, ex_recv.at[3 * n]).wait()
        total = row_in[n, 0]
        for i in range(1, XS):
            total = total + row_in[n, i]
        row_sum[n] = total
        for i in range(1, ys):
            pltpu.make_async_remote_copy(
                src_ref=row_sum.at[n], dst_ref=col_in.at[n, y], send_sem=ex_send.at[3 * n + 1],
                recv_sem=ex_recv.at[3 * n + 1],
                device_id={"ctx": lax.rem(y + i, ys) * XS + x}, device_id_type=MESH,
            ).start()
        col_in[n, y] = total

    def stage_back(n):
        rest = col_in.at[n, pl.ds(0, ys - 1)]
        pltpu.make_async_copy(rest, rest, ex_recv.at[3 * n + 1]).wait()
        zero = jnp.zeros((quarter, dim), F32)
        part = zero
        for i in range(ys):
            keep = (i > y) if n else (i < y)
            part = part + jnp.where(keep, col_in[n, i], zero)
        if n:
            grand = col_in[n, 0]
            for i in range(1, ys):
                grand = grand + col_in[n, i]
        members = range(XS - 1, -1, -1) if n else range(XS)
        for m in members:
            back_out[n, m, 0] = part
            if n:
                back_out[n, m, 1] = grand
            part = part + row_in[n, m]
        planes = 2 if n else 1
        for i in range(1, XS):
            send_x(
                3 * n + 2, lambda to: back_out.at[n, to, pl.ds(0, planes)],
                back_in.at[n, x, pl.ds(0, planes)], i,
            )
        back_in[n, x, 0] = back_out[n, x, 0]
        if n:
            back_in[n, x, 1] = back_out[n, x, 1]

    def stage_done(n):
        planes = 2 if n else 1
        three = back_in.at[n, pl.ds(0, XS - 1), pl.ds(0, planes)]
        pltpu.make_async_copy(three, three, ex_recv.at[3 * n + 2]).wait()

    total = jnp.zeros((dim, dim), F32)
    for b in range(blocks):
        at = pl.ds(b * SPAN, SPAN)
        kv_blk[b] = total
        total = total + dot(k_all[at], v_all[at], 0, 0)
    stage_quarters(0, total)

    def inner_query_grad(b):
        at = block_rows(b)
        qgrad_part[at] = dot(errors[b], k_all[at], 1, 0)

    inner_query_grad(0)
    inner_query_grad(1)
    stage_rows(0)
    inner_query_grad(2)
    inner_query_grad(3)
    stage_back(0)
    stage_done(0)
    state_in = s_own[0] + back_in[0, :, 0].reshape(dim, dim)
    for b in range(blocks):
        kv_blk[b] = kv_blk[b] + state_in

    def attend(b):
        at = block_rows(b)
        pltpu.make_async_copy(q_all.at[at], q_all.at[at], q_sem.at[b]).wait()
        q_b = q_all[at]
        low = jnp.where(causal, dot(q_b, k_all[at], 1, 1), 0.0).astype(BF16)
        scores[b] = low
        out = dot(q_b, kv_blk[b].astype(BF16), 1, 0) + dot(low, v_all[at], 1, 0)
        att_send[at] = (scale * out).astype(BF16)

    def give_back(owner):
        pltpu.make_async_remote_copy(
            src_ref=att_send.at[pl.ds(pl.multiple_of(owner * rows, rows), rows)],
            dst_ref=att_recv.at[me], send_sem=send_sem.at[2], recv_sem=att_sem,
            device_id={"head": owner}, device_id_type=MESH,
        ).start()

    def state_of_queries(b):
        at = block_rows(b)
        qg_blk[b] = dot(q_all[at], g_all[at], 0, 0)

    attend(my_block)
    place = lax.rem(me, per_block)

    @pl.loop(1, per_block)
    def _(j):
        give_back(my_block * per_block + lax.rem(place + j, per_block))

    pltpu.make_async_copy(att_send.at[my_rows], att_recv.at[me], att_sem).start()
    state_of_queries(my_block)

    low_side = lax.div(place, per_block // 2)

    @pl.loop(1, blocks)
    def _(i):
        step = jnp.where(i == 1, 2 * low_side - 1, jnp.where(i == 2, 1 - 2 * low_side, 2))
        b = lax.rem(my_block + step + blocks, blocks)
        attend(b)

        @pl.loop(0, per_block)
        def _(j):
            give_back(b * per_block + j)

        state_of_queries(b)

    total = jnp.zeros((dim, dim), F32)
    for b in range(blocks - 1, -1, -1):
        own = qg_blk[b]
        qg_blk[b] = total
        total = total + own
    stage_quarters(1, total)

    def inner_grads(b):
        at = block_rows(b)
        kgrad_part[at] = dot(errors[b], q_all[at], 0, 0)
        vgrad_part[at] = dot(scores[b], g_all[at], 0, 0)

    def query_grad(b):
        at = block_rows(b)
        out = dot(g_all[at], kv_blk[b].astype(BF16), 1, 1) + qgrad_part[at]
        qgrad_out[at] = (scale * out).astype(BF16)

    inner_grads(0)
    inner_grads(1)
    stage_rows(1)
    inner_grads(2)
    inner_grads(3)
    for b in range(blocks):
        query_grad(b)
    stage_back(1)
    stage_done(1)
    after = back_in[1, :, 0].reshape(dim, dim)
    sgrad_out[0] = scale * back_in[1, :, 1].reshape(dim, dim)
    for b in range(blocks):
        at = pl.ds(b * SPAN, SPAN)
        low = (after + qg_blk[b]).astype(BF16)
        kgrad_out[at] = (scale * (dot(v_all[at], low, 1, 1) + kgrad_part[at])).astype(BF16)
        vgrad_out[at] = (scale * (dot(k_all[at], low, 1, 0) + vgrad_part[at])).astype(BF16)

    pltpu.make_async_copy(att_recv, att_recv, att_sem).wait()
    for h in range(heads):
        att_out[:, h * dim : (h + 1) * dim] = att_recv[h]

    others = pl.ds(0, heads - 1)
    pltpu.make_async_copy(k_send.at[others], k_send.at[others], send_sem.at[0]).wait()
    pltpu.make_async_copy(q_send.at[others], q_send.at[others], send_sem.at[1]).wait()
    pltpu.make_async_copy(att_recv.at[others], att_recv.at[others], send_sem.at[2]).wait()
    for n in range(2):
        three = row_in.at[n, pl.ds(0, XS - 1)]
        pltpu.make_async_copy(three, three, ex_send.at[3 * n]).wait()
        rest = col_in.at[n, pl.ds(0, ys - 1)]
        pltpu.make_async_copy(rest, rest, ex_send.at[3 * n + 1]).wait()
        three = back_in.at[n, pl.ds(0, XS - 1), pl.ds(0, 2 if n else 1)]
        pltpu.make_async_copy(three, three, ex_send.at[3 * n + 2]).wait()


def local(zs, ys, query_rows, key_rows, value_rows, out_grad, entry_state):
    rows, features = query_rows.shape
    length, dim = value_rows.shape
    heads = 2 * zs
    blocks = length // SPAN
    scale = 1.0 / math.sqrt(dim * length * ys * XS)
    quarter = dim // XS
    any_spec = pl.BlockSpec(memory_space=pl.ANY)
    vmem_spec = pl.BlockSpec(memory_space=pltpu.VMEM)
    dma = pltpu.SemaphoreType.DMA
    wide = (length, dim)
    return pl.pallas_call(
        functools.partial(kernel, (zs, ys, rows, dim, blocks, scale)),
        out_shape=(
            jax.ShapeDtypeStruct((rows, features), BF16),
            jax.ShapeDtypeStruct(wide, BF16),
            jax.ShapeDtypeStruct(wide, BF16),
            jax.ShapeDtypeStruct(wide, BF16),
            jax.ShapeDtypeStruct((1, dim, dim), F32),
        ),
        in_specs=[any_spec] * 5,
        out_specs=[vmem_spec] * 5,
        scratch_shapes=[
            pltpu.VMEM((heads, rows, dim), BF16),
            pltpu.VMEM((heads, rows, dim), BF16),
            pltpu.VMEM(wide, BF16),
            pltpu.VMEM(wide, BF16),
            pltpu.VMEM(wide, BF16),
            pltpu.VMEM(wide, BF16),
            pltpu.VMEM((1, dim, dim), F32),
            pltpu.VMEM(wide, BF16),
            pltpu.VMEM((heads, rows, dim), BF16),
            pltpu.VMEM((blocks, SPAN, SPAN), BF16),
            pltpu.VMEM((blocks, SPAN, SPAN), BF16),
            pltpu.VMEM((blocks, dim, dim), F32),
            pltpu.VMEM((blocks, dim, dim), F32),
            pltpu.VMEM(wide, F32),
            pltpu.VMEM(wide, F32),
            pltpu.VMEM(wide, F32),
            pltpu.VMEM((2, XS, quarter, dim), F32),
            pltpu.VMEM((2, XS, quarter, dim), F32),
            pltpu.VMEM((2, quarter, dim), F32),
            pltpu.VMEM((2, ys, quarter, dim), F32),
            pltpu.VMEM((2, XS, 2, quarter, dim), F32),
            pltpu.VMEM((2, XS, 2, quarter, dim), F32),
            dma((5,)),
            dma((3,)),
            dma((blocks,)),
            dma((blocks,)),
            dma,
            dma((6,)),
            dma((6,)),
        ],
        compiler_params=pltpu.CompilerParams(
            collective_id=0, has_side_effects=True, vmem_limit_bytes=40 * 1024 * 1024
        ),
        name="layer",
    )(query_rows, key_rows, value_rows, out_grad, entry_state)


def solution(mesh):
    ys = mesh.shape["ctx"] // XS
    zs = mesh.shape["head"] // 2
    tokens = P(("ctx", "head"), None)
    split = P("ctx", "head")
    state = P("head", None, None)
    return jax.shard_map(
        functools.partial(local, zs, ys),
        mesh=mesh,
        in_specs=(tokens, tokens, split, split, state),
        out_specs=(tokens, split, split, split, state),
        check_vma=False,
    )
```

time: 223 us -> 91 us (0.41)
  the two profiles are of different devices: /device:TPU:94 before, /device:TPU:1 now
where the time goes in v1:
time: 91 us; the launch traced here: 90.6 us
  Pallas kernels  81.5 us (90%)
  local copies, waits for them, and re-layouts  8.43 us (9%)
    pallas_call x1, Pallas kernels, local(): pl.pallas_call(functools.partial(kernel, (zs, ys, rows, dim, blocks, scal...  81.5 us
    unnamed x15, local copies, waits for them, and re-layouts  8.43 us

profile of v1, /device:TPU:1, one launch (start us, length us, event | category | flops | bytes accessed | tf_op | source)
XLA Modules:
  0.0 90.6 jit_solution(6928638293128924343)
XLA Ops:
  0.6 0.0 copy-start
  0.6 1.0 %copy-done = bf16[48,4096]{1,0:T(8,128)(2,1)S(1)} copy-done((bf16[48,4096]{1,0:T(8,128)(2,1)S(1)}, bf16[48,4096]{1,0:T(8,128)(2,1)}, u32[]{:S(2)}) %copy-start) | copy-done | bytes 393240
  1.6 0.0 copy-start.1
  1.6 1.0 %copy-done.1 = bf16[48,4096]{1,0:T(8,128)(2,1)S(1)} copy-done((bf16[48,4096]{1,0:T(8,128)(2,1)S(1)}, bf16[48,4096]{1,0:T(8,128)(2,1)}, u32[]{:S(2)}) %copy-start.1) | copy-done | bytes 393240
  2.6 0.0 copy-start.2
  2.6 1.0 %copy-done.2 = bf16[1536,128]{1,0:T(8,128)(2,1)S(1)} copy-done((bf16[1536,128]{1,0:T(8,128)(2,1)S(1)}, bf16[1536,128]{1,0:T(8,128)(2,1)}, u32[]{:S(2)}) %copy-start.2) | copy-done | bytes 393240
  3.6 0.0 copy-start.3
  3.6 1.0 %copy-done.3 = bf16[1536,128]{1,0:T(8,128)(2,1)S(1)} copy-done((bf16[1536,128]{1,0:T(8,128)(2,1)S(1)}, bf16[1536,128]{1,0:T(8,128)(2,1)}, u32[]{:S(2)}) %copy-start.3) | copy-done | bytes 393240
  4.6 0.0 copy-start.4
  4.6 0.8 copy-done.4
  5.5 81.5 %layer.1 = (bf16[48,4096]{1,0:T(8,128)(2,1)S(1)}, bf16[1536,128]{1,0:T(8,128)(2,1)S(1)}, bf16[1536,128]{1,0:T(8,128)(2,1)S(1)}, bf16[1536,128]{1,0:T(8,128)(2,1)S(1)}, f32[1,128,128]{2,1,0:T(8,128)S(1)}) custom-call(bf16[48,4096]{1,0:T(8,128)(2,1)S(1)} %copy-done, bf16[48,4096]{1,0:T(8,128)(2,1)S(1)} %copy-done.1, bf16[1536,128]{1,0:T(8,128)(2,1)S(1)} %copy-done.2, ...), custom_call_target="tpu_custom_call" | custom-call | tf_op jit(solution)/shard_map/layer/pallas_call | solution.py:312
  87.0 0.7 copy.15
  87.8 0.7 copy.16
  88.5 0.7 copy.17
  89.2 0.7 copy.18
  90.0 0.6 copy.19
Async XLA Ops:
  0.6 1.0 %copy-start = (bf16[48,4096]{1,0:T(8,128)(2,1)S(1)}, bf16[48,4096]{1,0:T(8,128)(2,1)}, u32[]{:S(2)}) copy-start(bf16[48,4096]{1,0:T(8,128)(2,1)} %q_hbm.1) | copy-start | bytes 1179652
  1.6 1.0 %copy-start.1 = (bf16[48,4096]{1,0:T(8,128)(2,1)S(1)}, bf16[48,4096]{1,0:T(8,128)(2,1)}, u32[]{:S(2)}) copy-start(bf16[48,4096]{1,0:T(8,128)(2,1)} %k_hbm.1) | copy-start | bytes 1179652
  2.6 1.0 %copy-start.2 = (bf16[1536,128]{1,0:T(8,128)(2,1)S(1)}, bf16[1536,128]{1,0:T(8,128)(2,1)}, u32[]{:S(2)}) copy-start(bf16[1536,128]{1,0:T(8,128)(2,1)} %v_hbm.1) | copy-start | bytes 1179652
  3.6 1.0 %copy-start.3 = (bf16[1536,128]{1,0:T(8,128)(2,1)S(1)}, bf16[1536,128]{1,0:T(8,128)(2,1)}, u32[]{:S(2)}) copy-start(bf16[1536,128]{1,0:T(8,128)(2,1)} %g_hbm.1) | copy-start | bytes 1179652
  4.6 0.8 copy-start.4

commit v2 on v1

--- a/solution.py
+++ b/solution.py
@@ -10,6 +10,7 @@
 
 SPAN = 384
 XS = 4
+FAR_X = (2, 1, 3)
 MESH = pl.DeviceIdType.MESH
 F32 = jnp.float32
 BF16 = jnp.bfloat16
@@ -48,45 +49,57 @@
     def block_rows(b):
         return pl.ds(pl.multiple_of(b * SPAN, SPAN), SPAN)
 
-    for src, dst, sem in ((k_hbm, k_send, 0), (q_hbm, q_send, 1)):
+    barrier = pltpu.get_barrier_semaphore()
+
+    def greet(where):
+        pl.semaphore_signal(barrier, inc=1, device_id=where, device_id_type=MESH)
+
+    def chip_at(i):
+        step = lax.div(i + 1, 2) * (2 * lax.rem(i, 2) - 1)
+        return lax.rem(z + step + zs, zs)
+
+    @pl.loop(1, zs)
+    def _(i):
+        far = chip_at(zs - i)
+        greet({"head": 2 * far})
+        greet({"head": 2 * far + 1})
+
+    greet({"head": 2 * z + 1 - core})
+
+    @pl.loop(1, XS)
+    def _(i):
+        greet({"ctx": y * XS + lax.rem(x + i, XS)})
+
+    @pl.loop(1, ys)
+    def _(i):
+        greet({"ctx": lax.rem(y + i, ys) * XS + x})
+
+    def load_pieces(src, dst, sem):
         @pl.loop(0, heads)
         def _(h):
             pltpu.make_async_copy(src.at[:, columns(h)], dst.at[h], load_sem.at[sem]).start()
-    pltpu.make_async_copy(k_hbm.at[:, columns(me)], k_all.at[my_rows], k_sem.at[my_block]).start()
-    pltpu.make_async_copy(q_hbm.at[:, columns(me)], q_all.at[my_rows], q_sem.at[my_block]).start()
+
     load_v = pltpu.make_async_copy(v_hbm, v_all, load_sem.at[2])
     load_g = pltpu.make_async_copy(g_hbm, g_all, load_sem.at[3])
     load_s = pltpu.make_async_copy(s_hbm, s_own, load_sem.at[4])
-    load_v.start()
-    load_g.start()
-    load_s.start()
-
-    barrier = pltpu.get_barrier_semaphore()
-
-    @pl.loop(1, heads)
-    def _(i):
-        pl.semaphore_signal(
-            barrier, inc=1, device_id={"head": lax.rem(me + i, heads)}, device_id_type=MESH
-        )
-
-    @pl.loop(1, XS)
-    def _(i):
-        pl.semaphore_signal(
-            barrier, inc=1, device_id={"ctx": y * XS + lax.rem(x + i, XS)}, device_id_type=MESH
-        )
-
-    @pl.loop(1, ys)
-    def _(i):
-        pl.semaphore_signal(
-            barrier, inc=1, device_id={"ctx": lax.rem(y + i, ys) * XS + x}, device_id_type=MESH
-        )
-
-    pltpu.make_async_copy(k_send, k_send, load_sem.at[0]).wait()
-    pltpu.make_async_copy(q_send, q_send, load_sem.at[1]).wait()
-    load_v.wait()
-    load_g.wait()
-    load_s.wait()
-    pl.semaphore_wait(barrier, heads - 1 + XS - 1 + ys - 1)
+    with jax.named_scope("loads"):
+        load_v.start()
+        load_g.start()
+        load_pieces(k_hbm, k_send, 0)
+        pltpu.make_async_copy(k_hbm.at[:, columns(me)], k_all.at[my_rows], k_sem.at[my_block]).start()
+        load_pieces(q_hbm, q_send, 1)
+        pltpu.make_async_copy(q_hbm.at[:, columns(me)], q_all.at[my_rows], q_sem.at[my_block]).start()
+        load_s.start()
+
+    causal = lax.broadcasted_iota(jnp.int32, (SPAN, SPAN), 0) >= lax.broadcasted_iota(
+        jnp.int32, (SPAN, SPAN), 1
+    )
+
+    with jax.named_scope("loadwait"):
+        pltpu.make_async_copy(k_send, k_send, load_sem.at[0]).wait()
+        pltpu.make_async_copy(q_send, q_send, load_sem.at[1]).wait()
+    with jax.named_scope("barrier"):
+        pl.semaphore_wait(barrier, heads - 1 + XS - 1 + ys - 1)
 
     def post(src, dst, sem, recv, peer):
         pltpu.make_async_remote_copy(
@@ -94,31 +107,45 @@
             recv_sem=recv.at[my_block], device_id={"head": peer}, device_id_type=MESH,
         ).start()
 
-    for src, dst, sem, recv in ((k_send, k_all, 0, k_sem), (q_send, q_all, 1, q_sem)):
-        post(src, dst, sem, recv, 2 * z + 1 - core)
-
+    def post_all(src, dst, sem, recv, late=None):
         @pl.loop(1, zs)
         def _(i):
-            step = lax.div(i + 1, 2) * (2 * lax.rem(i, 2) - 1)
-            peer_z = lax.rem(z + step + zs, zs)
-            post(src, dst, sem, recv, 2 * peer_z + core)
-            post(src, dst, sem, recv, 2 * peer_z + 1 - core)
-
-    causal = lax.broadcasted_iota(jnp.int32, (SPAN, SPAN), 0) >= lax.broadcasted_iota(
-        jnp.int32, (SPAN, SPAN), 1
-    )
-
-    @pl.loop(0, blocks)
-    def _(b):
-        at = block_rows(b)
-        errors[b] = jnp.where(causal, dot(g_all[at], v_all[at], 1, 1), 0.0).astype(BF16)
-
-    for b in range(blocks):
+            peer_z = chip_at(zs - i)
+
+            def both():
+                post(src, dst, sem, recv, 2 * peer_z + core)
+                post(src, dst, sem, recv, 2 * peer_z + 1 - core)
+
+            if late is None:
+                both()
+            else:
+                pl.when(lax.div(peer_z, zs // 2) == late)(both)
+
+    with jax.named_scope("post"):
+        post_all(k_send, k_all, 0, k_sem)
+        post(k_send, k_all, 0, k_sem, 2 * z + 1 - core)
+
+    with jax.named_scope("errors"):
+        load_v.wait()
+        load_g.wait()
+        load_s.wait()
+
+        @pl.loop(0, blocks)
+        def _(b):
+            at = block_rows(b)
+            errors[b] = jnp.where(causal, dot(g_all[at], v_all[at], 1, 1), 0.0).astype(BF16)
+
+    def wait_k(b):
         pltpu.make_async_copy(
             k_all.at[pl.ds(b * SPAN, SPAN)], k_all.at[pl.ds(b * SPAN, SPAN)], k_sem.at[b]
         ).wait()
 
+    with jax.named_scope("kwait"):
+        for b in range(blocks):
+            wait_k(b)
+
     quarter = dim // XS
+    far_y = sorted(range(1, ys), key=lambda i: -min(i, ys - i))
 
     def send_x(which, src_of, dst, i):
         to = lax.rem(x + i, XS)
@@ -129,7 +156,7 @@
 
     def stage_quarters(n, total):
         own_quarter[n] = total.reshape(XS, quarter, dim)
-        for i in range(1, XS):
+        for i in FAR_X:
             send_x(3 * n, lambda to: own_quarter.at[n, to], row_in.at[n, x], i)
         row_in[n, x] = own_quarter[n, x]
 
@@ -140,7 +167,7 @@
         for i in range(1, XS):
             total = total + row_in[n, i]
         row_sum[n] = total
-        for i in range(1, ys):
+        for i in far_y:
             pltpu.make_async_remote_copy(
                 src_ref=row_sum.at[n], dst_ref=col_in.at[n, y], send_sem=ex_send.at[3 * n + 1],
                 recv_sem=ex_recv.at[3 * n + 1],
@@ -167,7 +194,7 @@
                 back_out[n, m, 1] = grand
             part = part + row_in[n, m]
         planes = 2 if n else 1
-        for i in range(1, XS):
+        for i in FAR_X:
             send_x(
                 3 * n + 2, lambda to: back_out.at[n, to, pl.ds(0, planes)],
                 back_in.at[n, x, pl.ds(0, planes)], i,
@@ -186,31 +213,44 @@
         at = pl.ds(b * SPAN, SPAN)
         kv_blk[b] = total
         total = total + dot(k_all[at], v_all[at], 0, 0)
-    stage_quarters(0, total)
+    with jax.named_scope("kvq"):
+        stage_quarters(0, total)
+
+    with jax.named_scope("postq"):
+        post_all(q_send, q_all, 1, q_sem, 0)
+        post_all(q_send, q_all, 1, q_sem, 1)
+        post(q_send, q_all, 1, q_sem, 2 * z + 1 - core)
 
     def inner_query_grad(b):
         at = block_rows(b)
         qgrad_part[at] = dot(errors[b], k_all[at], 1, 0)
 
-    inner_query_grad(0)
-    inner_query_grad(1)
-    stage_rows(0)
-    inner_query_grad(2)
-    inner_query_grad(3)
-    stage_back(0)
-    stage_done(0)
+    with jax.named_scope("iqg01"):
+        inner_query_grad(0)
+        inner_query_grad(1)
+    with jax.named_scope("rows0"):
+        stage_rows(0)
+    with jax.named_scope("iqg23"):
+        inner_query_grad(2)
+        inner_query_grad(3)
+    with jax.named_scope("back0"):
+        stage_back(0)
+    with jax.named_scope("done0"):
+        stage_done(0)
     state_in = s_own[0] + back_in[0, :, 0].reshape(dim, dim)
     for b in range(blocks):
         kv_blk[b] = kv_blk[b] + state_in
 
     def attend(b):
         at = block_rows(b)
-        pltpu.make_async_copy(q_all.at[at], q_all.at[at], q_sem.at[b]).wait()
-        q_b = q_all[at]
-        low = jnp.where(causal, dot(q_b, k_all[at], 1, 1), 0.0).astype(BF16)
-        scores[b] = low
-        out = dot(q_b, kv_blk[b].astype(BF16), 1, 0) + dot(low, v_all[at], 1, 0)
-        att_send[at] = (scale * out).astype(BF16)
+        with jax.named_scope("qwait"):
+            pltpu.make_async_copy(q_all.at[at], q_all.at[at], q_sem.at[b]).wait()
+        with jax.named_scope("attend"):
+            q_b = q_all[at]
+            low = jnp.where(causal, dot(q_b, k_all[at], 1, 1), 0.0).astype(BF16)
+            scores[b] = low
+            out = dot(q_b, kv_blk[b].astype(BF16), 1, 0) + dot(low, v_all[at], 1, 0)
+            att_send[at] = (scale * out).astype(BF16)
 
     def give_back(owner):
         pltpu.make_async_remote_copy(
@@ -221,38 +261,33 @@
 
     def state_of_queries(b):
         at = block_rows(b)
-        qg_blk[b] = dot(q_all[at], g_all[at], 0, 0)
-
-    attend(my_block)
-    place = lax.rem(me, per_block)
-
-    @pl.loop(1, per_block)
-    def _(j):
-        give_back(my_block * per_block + lax.rem(place + j, per_block))
-
-    pltpu.make_async_copy(att_send.at[my_rows], att_recv.at[me], att_sem).start()
-    state_of_queries(my_block)
-
-    low_side = lax.div(place, per_block // 2)
-
-    @pl.loop(1, blocks)
+        with jax.named_scope("qg"):
+            qg_blk[b] = dot(q_all[at], g_all[at], 0, 0)
+
+    @pl.loop(0, blocks)
     def _(i):
-        step = jnp.where(i == 1, 2 * low_side - 1, jnp.where(i == 2, 1 - 2 * low_side, 2))
-        b = lax.rem(my_block + step + blocks, blocks)
+        b = i
         attend(b)
 
         @pl.loop(0, per_block)
         def _(j):
-            give_back(b * per_block + j)
+            owner = b * per_block + j
+
+            @pl.when(owner != me)
+            def _():
+                give_back(owner)
 
         state_of_queries(b)
+
+    pltpu.make_async_copy(att_send.at[my_rows], att_recv.at[me], att_sem).start()
 
     total = jnp.zeros((dim, dim), F32)
     for b in range(blocks - 1, -1, -1):
         own = qg_blk[b]
         qg_blk[b] = total
         total = total + own
-    stage_quarters(1, total)
+    with jax.named_scope("qgq"):
+        stage_quarters(1, total)
 
     def inner_grads(b):
         at = block_rows(b)
@@ -264,15 +299,21 @@
         out = dot(g_all[at], kv_blk[b].astype(BF16), 1, 1) + qgrad_part[at]
         qgrad_out[at] = (scale * out).astype(BF16)
 
-    inner_grads(0)
-    inner_grads(1)
-    stage_rows(1)
-    inner_grads(2)
-    inner_grads(3)
-    for b in range(blocks):
-        query_grad(b)
-    stage_back(1)
-    stage_done(1)
+    with jax.named_scope("ig01"):
+        inner_grads(0)
+        inner_grads(1)
+    with jax.named_scope("rows1"):
+        stage_rows(1)
+    with jax.named_scope("ig23"):
+        inner_grads(2)
+        inner_grads(3)
+    with jax.named_scope("qgrad"):
+        for b in range(blocks):
+            query_grad(b)
+    with jax.named_scope("back1"):
+        stage_back(1)
+    with jax.named_scope("done1"):
+        stage_done(1)
     after = back_in[1, :, 0].reshape(dim, dim)
     sgrad_out[0] = scale * back_in[1, :, 1].reshape(dim, dim)
     for b in range(blocks):
@@ -281,7 +322,8 @@
         kgrad_out[at] = (scale * (dot(v_all[at], low, 1, 1) + kgrad_part[at])).astype(BF16)
         vgrad_out[at] = (scale * (dot(k_all[at], low, 1, 0) + vgrad_part[at])).astype(BF16)
 
-    pltpu.make_async_copy(att_recv, att_recv, att_sem).wait()
+    with jax.named_scope("attwait"):
+        pltpu.make_async_copy(att_recv, att_recv, att_sem).wait()
     for h in range(heads):
         att_out[:, h * dim : (h + 1) * dim] = att_recv[h]
 
@@ -298,6 +340,15 @@
         pltpu.make_async_copy(three, three, ex_send.at[3 * n + 2]).wait()
 
 
+def write_out(*refs):
+    sem = refs[-1]
+    copies = [pltpu.make_async_copy(refs[i], refs[5 + i], sem.at[i]) for i in range(5)]
+    for copy in copies:
+        copy.start()
+    for copy in copies:
+        copy.wait()
+
+
 def local(zs, ys, query_rows, key_rows, value_rows, out_grad, entry_state):
     rows, features = query_rows.shape
     length, dim = value_rows.shape
@@ -306,10 +357,11 @@
     scale = 1.0 / math.sqrt(dim * length * ys * XS)
     quarter = dim // XS
     any_spec = pl.BlockSpec(memory_space=pl.ANY)
+    hbm_spec = pl.BlockSpec(memory_space=pltpu.HBM)
     vmem_spec = pl.BlockSpec(memory_space=pltpu.VMEM)
     dma = pltpu.SemaphoreType.DMA
     wide = (length, dim)
-    return pl.pallas_call(
+    results = pl.pallas_call(
         functools.partial(kernel, (zs, ys, rows, dim, blocks, scale)),
         out_shape=(
             jax.ShapeDtypeStruct((rows, features), BF16),
@@ -318,7 +370,7 @@
             jax.ShapeDtypeStruct(wide, BF16),
             jax.ShapeDtypeStruct((1, dim, dim), F32),
         ),
-        in_specs=[any_spec] * 5,
+        in_specs=[hbm_spec] * 5,
         out_specs=[vmem_spec] * 5,
         scratch_shapes=[
             pltpu.VMEM((heads, rows, dim), BF16),
@@ -355,7 +407,16 @@
             collective_id=0, has_side_effects=True, vmem_limit_bytes=40 * 1024 * 1024
         ),
         name="layer",
-    )(query_rows, key_rows, value_rows, out_grad, entry_state)
+    )(*(pltpu.with_memory_space_constraint(a, pltpu.HBM) for a in (query_rows, key_rows, value_rows, out_grad, entry_state)))
+    return pl.pallas_call(
+        write_out,
+        out_shape=tuple(jax.ShapeDtypeStruct(r.shape, r.dtype) for r in results),
+        in_specs=[vmem_spec] * 5,
+        out_specs=[hbm_spec] * 5,
+        scratch_shapes=[dma((5,))],
+        compiler_params=pltpu.CompilerParams(vmem_limit_bytes=16 * 1024 * 1024),
+        name="write_out",
+    )(*results)
 
 
 def solution(mesh):

time: 91 us -> 78 us (0.86); the launches traced: 90.6 us -> 76.4 us
  local copies, waits for them, and re-layouts: 8.43 us -> 0 us
  Pallas kernels: 81.5 us -> 75.8 us
    unnamed x15 -> x0, local copies, waits for them, and re-layouts: 8.43 us -> none
    pallas_call x1, Pallas kernels: 81.5 us -> 74.6 us  [local(): pl.pallas_call(functools.partial(kernel, (zs, ys, rows, dim, blocks, scal...]
    pallas_call x0 -> x1, Pallas kernels: none -> 1.19 us  [local(): pl.pallas_call(write_out, out_shape=tuple((jax.ShapeDtypeStruct(r.shape,...]
where the time goes in v2:
time: 78 us; the launch traced here: 76.4 us
  Pallas kernels  75.8 us (97%)
    pallas_call x1, Pallas kernels, local(): pl.pallas_call(functools.partial(kernel, (zs, ys, rows, dim, blocks, scal...  74.6 us

profile of v2, /device:TPU:1, one launch (start us, length us, event | category | flops | bytes accessed | tf_op | source)
XLA Modules:
  0.0 76.4 jit_solution(8348631775822041125)
XLA Ops:
  0.6 74.6 %layer.1 = (bf16[48,4096]{1,0:T(8,128)(2,1)S(1)}, bf16[1536,128]{1,0:T(8,128)(2,1)S(1)}, bf16[1536,128]{1,0:T(8,128)(2,1)S(1)}, bf16[1536,128]{1,0:T(8,128)(2,1)S(1)}, f32[1,128,128]{2,1,0:T(8,128)S(1)}) custom-call(bf16[48,4096]{1,0:T(8,128)(2,1)} %q_hbm.1, bf16[48,4096]{1,0:T(8,128)(2,1)} %k_hbm.1, bf16[1536,128]{1,0:T(8,128)(2,1)} %v_hbm.1, ...), custom_call_target="tpu_custom_call" | custom-call | tf_op jit(solution)/shard_map/layer/pallas_call | solution.py:364
  75.2 1.2 %write_out.1 = (bf16[48,4096]{1,0:T(8,128)(2,1)}, bf16[1536,128]{1,0:T(8,128)(2,1)}, bf16[1536,128]{1,0:T(8,128)(2,1)}, bf16[1536,128]{1,0:T(8,128)(2,1)}, f32[1,128,128]{2,1,0:T(8,128)}) custom-call(bf16[48,4096]{1,0:T(8,128)(2,1)S(1)} %get-tuple-element.10.refs_0_, bf16[1536,128]{1,0:T(8,128)(2,1)S(1)} %get-tuple-element.11.refs_1_, ...), custom_call_target="tpu_custom_call" | custom-call | tf_op jit(solution)/shard_map/write_out/pallas_call | solution.py:411

commit v3 on v2

--- a/solution.py
+++ b/solution.py
@@ -137,12 +137,22 @@
 
     def wait_k(b):
         pltpu.make_async_copy(
-            k_all.at[pl.ds(b * SPAN, SPAN)], k_all.at[pl.ds(b * SPAN, SPAN)], k_sem.at[b]
+            k_all.at[block_rows(b)], k_all.at[block_rows(b)], k_sem.at[b]
         ).wait()
 
+    my_half = lax.div(z, zs // 2)
+
+    def wait_half(h):
+        @pl.loop(0, blocks // 2)
+        def _(i):
+            wait_k(h * (blocks // 2) + i)
+
     with jax.named_scope("kwait"):
-        for b in range(blocks):
-            wait_k(b)
+        wait_half(my_half)
+    with jax.named_scope("postq"):
+        post_all(q_send, q_all, 1, q_sem, 0)
+    with jax.named_scope("kwait"):
+        wait_half(1 - my_half)
 
     quarter = dim // XS
     far_y = sorted(range(1, ys), key=lambda i: -min(i, ys - i))
@@ -217,7 +227,6 @@
         stage_quarters(0, total)
 
     with jax.named_scope("postq"):
-        post_all(q_send, q_all, 1, q_sem, 0)
         post_all(q_send, q_all, 1, q_sem, 1)
         post(q_send, q_all, 1, q_sem, 2 * z + 1 - core)
 

time: 78 us -> 76.5 us (0.981)
  Pallas kernels: 75.8 us -> 74.5 us
    pallas_call x1, Pallas kernels: 74.6 us -> 73.3 us  [local(): pl.pallas_call(functools.partial(kernel, (zs, ys, rows, dim, blocks, scal...]
where the time goes in v3:
time: 76.5 us; the launch traced here: 75.2 us
  Pallas kernels  74.5 us (97%)
    pallas_call x1, Pallas kernels, local(): pl.pallas_call(functools.partial(kernel, (zs, ys, rows, dim, blocks, scal...  73.3 us

profile of v3, /device:TPU:1, one launch (start us, length us, event | category | flops | bytes accessed | tf_op | source)
XLA Modules:
  0.0 75.2 jit_solution(9502065007911941191)
XLA Ops:
  0.6 73.3 %layer.1 = (bf16[48,4096]{1,0:T(8,128)(2,1)S(1)}, bf16[1536,128]{1,0:T(8,128)(2,1)S(1)}, bf16[1536,128]{1,0:T(8,128)(2,1)S(1)}, bf16[1536,128]{1,0:T(8,128)(2,1)S(1)}, f32[1,128,128]{2,1,0:T(8,128)S(1)}) custom-call(bf16[48,4096]{1,0:T(8,128)(2,1)} %q_hbm.1, bf16[48,4096]{1,0:T(8,128)(2,1)} %k_hbm.1, bf16[1536,128]{1,0:T(8,128)(2,1)} %v_hbm.1, ...), custom_call_target="tpu_custom_call" | custom-call | tf_op jit(solution)/shard_map/layer/pallas_call | solution.py:373
  74.0 1.2 %write_out.1 = (bf16[48,4096]{1,0:T(8,128)(2,1)}, bf16[1536,128]{1,0:T(8,128)(2,1)}, bf16[1536,128]{1,0:T(8,128)(2,1)}, bf16[1536,128]{1,0:T(8,128)(2,1)}, f32[1,128,128]{2,1,0:T(8,128)}) custom-call(bf16[48,4096]{1,0:T(8,128)(2,1)S(1)} %get-tuple-element.10.refs_0_, bf16[1536,128]{1,0:T(8,128)(2,1)S(1)} %get-tuple-element.11.refs_1_, ...), custom_call_target="tpu_custom_call" | custom-call | tf_op jit(solution)/shard_map/write_out/pallas_call | solution.py:420
